TPU v7x, 32 devices: a whole 2x2x4 slice. The times are simulated.
32 devices in a mesh: heads: 4 (over y, x), seq: 8 (over z, core).
Axes of the slice: x: 2, y: 2, z: 4, core: 2. Of those that a mesh axis runs over, the one named last changes fastest.
Arguments:
- tokens: bfloat16 [7168, 2048], P('seq'), may hold values from -6 to 6
- w_qkv: bfloat16 [2048, 3, 2048], P(None, None, 'heads'), may hold values from -0.1875 to 0.1875
- w_out: bfloat16 [2048, 2048], P('heads'), may hold values from -0.75 to 0.75
- w_up: bfloat16 [2048, 8192], P('seq', 'heads'), may hold values from -0.125 to 0.125
- w_down: bfloat16 [8192, 2048], P('heads', 'seq'), may hold values from -0.0625 to 0.0625
- gain_attn: float32 [2048], replicated, may hold values from 0.1 to 1.9
- gain_ffn: float32 [2048], replicated, may hold values from 0.1 to 1.9
- w_router: float32 [2048, 8], replicated, may hold values from -0.25 to 0.25
- head_quarters: int32 [5], replicated, may hold values from 1 to 4, as said below
- ffn_quarters: int32 [5], replicated, may hold values from 1 to 4, as said below
- router_targets: int32 [5, 2], replicated, may hold values from 0 to 3
- cotangent: bfloat16 [7168, 2048], P('seq'), may hold values from -6 to 6
Outputs:
- output: bfloat16 [7168, 2048], P('seq')
- grad_tokens: float32 [7168, 2048], P('seq')
- grad_qkv: float32 [2048, 3, 2048], P(None, None, 'heads')
- grad_out: float32 [2048, 2048], P('heads')
- grad_up: float32 [2048, 8192], P('seq', 'heads')
- grad_down: float32 [8192, 2048], P('heads', 'seq')
- grad_gain_attn: float32 [2048], replicated
- grad_gain_ffn: float32 [2048], replicated
- grad_router: float32 [2048, 8], replicated
Inputs may be any that keep to these rules, and one draw needn't show every extreme that they name: Sequence s uses the first head_quarters[s] * 4 heads; some sequence uses all heads and some a quarter of them. Sequence s uses the first ffn_quarters[s] * 2048 hidden units; some sequence uses all and some a quarter.
All inputs are finite; a program needn't handle non-finite values.
Results may differ from a plain program's by a relative error of at most 0.023.
Values may be sent and summed in bfloat16 or wider, within the bound.
No kernel may reach another device: no remote copies, remote signals or barrier semaphores. Data moves between devices by JAX's collectives and lax.ppermute only.
A program may use at most 256 MiB of HBM per device.

v0:
```python
import jax
import jax.numpy as jnp
from jax import lax
from jax.sharding import PartitionSpec as P

D = 2048
H = 16
HD = 128
FF = 8192
SHORT_DEV = 128
NSHORT = 3
NLONG = 2
LEVELS = 4
SEQS = 5
epsilon = 1e-05
highest = lax.Precision.HIGHEST


def normalize_parts(values):
    centered = values - jnp.mean(values, axis=-1, keepdims=True)
    inverse = lax.rsqrt(jnp.mean(centered * centered, axis=-1, keepdims=True) + epsilon)
    return (centered * inverse, inverse)


def normalize_back(grad_normed, normed_hat, inverse, gain):
    grad_hat = grad_normed * gain
    middle = (
        grad_hat
        - jnp.mean(grad_hat, axis=-1, keepdims=True)
        - normed_hat * jnp.mean(grad_hat * normed_hat, axis=-1, keepdims=True)
    )
    return (inverse * middle, jnp.sum(grad_normed * normed_hat, axis=0))


def rotate(values, cosine, sine, inverse_turn):
    row_count = values.shape[0]
    shaped = values.reshape(row_count, -1, HD)
    half_dim = HD // 2
    former = shaped[..., :half_dim]
    latter = shaped[..., half_dim:]
    if inverse_turn:
        turned = [former * cosine + latter * sine, latter * cosine - former * sine]
    else:
        turned = [former * cosine - latter * sine, latter * cosine + former * sine]
    return jnp.concatenate(turned, axis=-1).reshape(row_count, -1)


def gather_rows(keys, values):
    return (
        lax.all_gather(keys, "seq", axis=1, tiled=True),
        lax.all_gather(values, "seq", axis=1, tiled=True),
    )


def masked_scores(query, keys, first_pos):
    seq_number, seq_size = (query.shape[0], query.shape[1])
    length = keys.shape[1]
    query_heads = query.reshape(seq_number, seq_size, -1, HD)
    key_heads = keys.reshape(seq_number, length, -1, HD)
    scores = jnp.einsum(
        "cqhd,ckhd->chqk", query_heads, key_heads, preferred_element_type=jnp.float32
    ) * HD ** (-0.5)
    allowed = jnp.arange(length)[None, :] <= (first_pos + jnp.arange(seq_size))[:, None]
    return (jnp.where(allowed[None, None], scores, -1e30), query_heads, key_heads)


def attend_forward(query, keys, values, first_pos):
    seq_number, seq_size = (query.shape[0], query.shape[1])
    scores, query_heads, key_heads = masked_scores(query, keys, first_pos)
    largest = jnp.max(scores, axis=-1, keepdims=True)
    raised = jnp.exp(scores - largest)
    total = jnp.sum(raised, axis=-1, keepdims=True)
    probs = (raised / total).astype(jnp.bfloat16)
    value_heads = values.reshape(seq_number, values.shape[1], -1, HD)
    mixed = jnp.einsum("chqk,ckhd->cqhd", probs, value_heads, preferred_element_type=jnp.float32)
    return (mixed.reshape(seq_number, seq_size, -1), largest + jnp.log(total))


def attend_backward(query, keys, values, grad_mixed, log_total, first_pos):
    seq_number, seq_size = (query.shape[0], query.shape[1])
    length = keys.shape[1]
    scores, query_heads, key_heads = masked_scores(query, keys, first_pos)
    probs = jnp.exp(scores - log_total)
    value_heads = values.reshape(seq_number, length, -1, HD)
    grad_heads = grad_mixed.reshape(seq_number, seq_size, -1, HD)
    grad_probs = jnp.einsum(
        "cqhd,ckhd->chqk", grad_heads, value_heads, preferred_element_type=jnp.float32
    )
    delta = jnp.sum(probs * grad_probs, axis=-1)
    grad_scores = (probs * (grad_probs - delta[..., None])).astype(jnp.bfloat16)
    grad_query = jnp.einsum(
        "chqk,ckhd->cqhd", grad_scores, key_heads, preferred_element_type=jnp.float32
    ) * HD ** (-0.5)
    grad_query = grad_query.reshape(seq_number, seq_size, -1)
    return (grad_query, delta)


def attend_key_side(query_all, keys, values, grad_all, total_all, delta_all, key_first):
    seq_number, length = (query_all.shape[0], query_all.shape[1])
    key_count = keys.shape[1]
    query_heads = query_all.reshape(seq_number, length, -1, HD)
    key_heads = keys.reshape(seq_number, key_count, -1, HD)
    value_heads = values.reshape(seq_number, key_count, -1, HD)
    grad_heads = grad_all.reshape(seq_number, length, -1, HD)
    scores = jnp.einsum(
        "cqhd,ckhd->chqk", query_heads, key_heads, preferred_element_type=jnp.float32
    ) * HD ** (-0.5)
    allowed = (key_first + jnp.arange(key_count))[None, :] <= jnp.arange(length)[:, None]
    scores = jnp.where(allowed[None, None], scores, -1e30)
    probs = jnp.exp(scores - total_all[..., None])
    probs_low = probs.astype(jnp.bfloat16)
    grad_probs = jnp.einsum(
        "cqhd,ckhd->chqk", grad_heads, value_heads, preferred_element_type=jnp.float32
    )
    grad_scores = (probs * (grad_probs - delta_all[..., None])).astype(jnp.bfloat16)
    grad_values = jnp.einsum(
        "chqk,cqhd->ckhd", probs_low, grad_heads, preferred_element_type=jnp.float32
    )
    grad_keys = jnp.einsum(
        "chqk,cqhd->ckhd", grad_scores, query_heads, preferred_element_type=jnp.float32
    ) * HD ** (-0.5)
    return (
        grad_keys.reshape(seq_number, key_count, -1),
        grad_values.reshape(seq_number, key_count, -1),
    )


def local(
    tokens,
    w_qkv,
    w_out,
    w_up,
    w_down,
    gain_attn,
    gain_ffn,
    w_router,
    head_quarters,
    ffn_quarters,
    router_targets,
    cotangent,
):
    row_count = tokens.shape[0]
    seq_rank = lax.axis_index("seq")
    seq_count = lax.axis_size("seq")
    head_rank = lax.axis_index("heads")
    head_width = w_out.shape[0]
    ffn_width = w_up.shape[1]
    short_rows = NSHORT * SHORT_DEV
    column = jnp.arange(row_count)
    is_short = column < short_rows
    offset = column - short_rows
    seq_id = jnp.where(is_short, column // SHORT_DEV, NSHORT + offset // (2 * SHORT_DEV))
    position = jnp.where(
        is_short,
        seq_rank * SHORT_DEV + column % SHORT_DEV,
        seq_rank * 2 * SHORT_DEV + offset % (2 * SHORT_DEV),
    )
    in_seq = seq_id[:, None] == jnp.arange(SEQS)[None, :]
    member = in_seq.astype(jnp.float32)
    seq_length = jnp.where(
        jnp.arange(SEQS) < NSHORT, SHORT_DEV * seq_count, 2 * SHORT_DEV * seq_count
    ).astype(jnp.float32)
    head_level = jnp.sum(jnp.where(in_seq, head_quarters[None, :], 0), axis=1)
    ffn_level = jnp.sum(jnp.where(in_seq, ffn_quarters[None, :], 0), axis=1)
    head_index = head_rank * (head_width // HD) + jnp.arange(head_width) // HD
    head_live = (head_index[None, :] < (head_level * (H // LEVELS))[:, None]).astype(jnp.bfloat16)
    unit_index = head_rank * ffn_width + jnp.arange(ffn_width)
    ffn_live = (unit_index[None, :] < (ffn_level * (FF // LEVELS))[:, None]).astype(jnp.float32)
    half_dim = HD // 2
    frequency = 10000.0 ** (-jnp.arange(half_dim, dtype=jnp.float32) * 2.0 / HD)
    angle = position.astype(jnp.float32)[:, None] * frequency[None, :]
    cosine = jnp.cos(angle)[:, None, :]
    sine = jnp.sin(angle)[:, None, :]
    tokens_wide = tokens.astype(jnp.float32)
    hat_one, inverse_one = normalize_parts(tokens_wide)
    normed_one = hat_one * gain_attn
    normed_low = normed_one.astype(jnp.bfloat16)
    flat_qkv = w_qkv.reshape(D, -1)
    projected = jnp.dot(normed_low, flat_qkv, preferred_element_type=jnp.float32).reshape(
        row_count, 3, head_width
    )
    query = rotate(projected[:, 0], cosine, sine, False).astype(jnp.bfloat16)
    keys = rotate(projected[:, 1], cosine, sine, False).astype(jnp.bfloat16)
    values = projected[:, 2].astype(jnp.bfloat16)
    partial_pool = jnp.dot(
        member.T, normed_one, precision=highest, preferred_element_type=jnp.float32
    )
    pooled = (
        lax.psum(partial_pool.astype(jnp.bfloat16), "seq").astype(jnp.float32)
        * lax.rsqrt(seq_length)[:, None]
    )
    shape_list = ((0, NSHORT, SHORT_DEV), (short_rows, NLONG, 2 * SHORT_DEV))
    saved_parts = []
    mixed_parts = []
    for row_start, seq_number, seq_size in shape_list:
        row_stop = row_start + seq_number * seq_size
        piece_query = query[row_start:row_stop].reshape(seq_number, seq_size, head_width)
        piece_keys = keys[row_start:row_stop].reshape(seq_number, seq_size, head_width)
        piece_values = values[row_start:row_stop].reshape(seq_number, seq_size, head_width)
        gathered_keys, gathered_values = gather_rows(piece_keys, piece_values)
        mixed, log_total = attend_forward(
            piece_query, gathered_keys, gathered_values, seq_rank * seq_size
        )
        saved_parts.append(
            (piece_query, piece_keys, piece_values, gathered_keys, gathered_values, log_total)
        )
        mixed_parts.append(mixed.reshape(seq_number * seq_size, head_width))
    heads_out = (jnp.concatenate(mixed_parts, axis=0) * head_live).astype(jnp.bfloat16)
    attn_part = jnp.dot(heads_out, w_out, preferred_element_type=jnp.float32)
    hidden = tokens_wide + lax.psum(attn_part, "heads")
    hat_two, inverse_two = normalize_parts(hidden)
    normed_two = (hat_two * gain_ffn).astype(jnp.bfloat16)
    full_up, full_down = (
        lax.all_gather(w_up, "seq", axis=0, tiled=True),
        lax.all_gather(w_down, "seq", axis=1, tiled=True),
    )
    upward = jnp.dot(normed_two, full_up, preferred_element_type=jnp.float32)
    active = (jnp.square(jnp.maximum(upward, 0.0)) * ffn_live).astype(jnp.bfloat16)
    ffn_part = jnp.dot(active, full_down, preferred_element_type=jnp.float32)
    output = (hidden + lax.psum(ffn_part.astype(jnp.bfloat16), "heads").astype(jnp.float32)).astype(
        jnp.bfloat16
    )
    back_up, back_down = (
        lax.all_gather(w_up, "seq", axis=0, tiled=True),
        lax.all_gather(w_down, "seq", axis=1, tiled=True),
    )
    upward_again = jnp.dot(normed_two, back_up, preferred_element_type=jnp.float32)
    active_again = (jnp.square(jnp.maximum(upward_again, 0.0)) * ffn_live).astype(jnp.bfloat16)
    grad_active = jnp.dot(cotangent, back_down.T, preferred_element_type=jnp.float32).astype(
        jnp.bfloat16
    )
    grad_upward = (
        grad_active.astype(jnp.float32) * ffn_live * 2.0 * jnp.maximum(upward_again, 0.0)
    ).astype(jnp.bfloat16)
    grad_down_part = jnp.dot(active_again.T, cotangent, preferred_element_type=jnp.float32)
    grad_up_part = jnp.dot(normed_two.T, grad_upward, preferred_element_type=jnp.float32)
    grad_two = lax.psum(
        jnp.dot(grad_upward, back_up.T, preferred_element_type=jnp.float32), "heads"
    )
    grad_up, grad_down = (
        lax.psum_scatter(
            grad_up_part.astype(jnp.bfloat16), "seq", scatter_dimension=0, tiled=True
        ).astype(jnp.float32),
        lax.psum_scatter(
            grad_down_part.astype(jnp.bfloat16), "seq", scatter_dimension=1, tiled=True
        ).astype(jnp.float32),
    )
    back_two, grad_gain_two = normalize_back(grad_two, hat_two, inverse_two, gain_ffn)
    grad_hidden = cotangent.astype(jnp.float32) + back_two
    grad_attn = grad_hidden.astype(jnp.bfloat16)
    grad_out_part = jnp.dot(heads_out.T, grad_attn, preferred_element_type=jnp.float32)
    grad_heads = (
        jnp.dot(grad_attn, w_out.T, preferred_element_type=jnp.float32).astype(jnp.bfloat16)
        * head_live
    )
    query_grads = []
    key_grads = []
    value_grads = []
    for shape_entry, saved in zip(shape_list, saved_parts):
        row_start, seq_number, seq_size = shape_entry
        piece_query, piece_keys, piece_values, gathered_keys, gathered_values, log_total = saved
        piece_grad = grad_heads[row_start : row_start + seq_number * seq_size].reshape(
            seq_number, seq_size, head_width
        )
        grad_query, delta = attend_backward(
            piece_query, gathered_keys, gathered_values, piece_grad, log_total, seq_rank * seq_size
        )
        query_all, grad_all = (
            lax.all_gather(piece_query, "seq", axis=1, tiled=True),
            lax.all_gather(piece_grad, "seq", axis=1, tiled=True),
        )
        total_all, delta_all = (
            lax.all_gather(log_total[..., 0], "seq", axis=2, tiled=True),
            lax.all_gather(delta, "seq", axis=2, tiled=True),
        )
        local_keys, local_values = attend_key_side(
            query_all, piece_keys, piece_values, grad_all, total_all, delta_all, seq_rank * seq_size
        )
        query_grads.append(grad_query.reshape(seq_number * seq_size, head_width))
        key_grads.append(local_keys.reshape(seq_number * seq_size, head_width))
        value_grads.append(local_values.reshape(seq_number * seq_size, head_width))
    grad_query_all = rotate(jnp.concatenate(query_grads, axis=0), cosine, sine, True)
    grad_key_all = rotate(jnp.concatenate(key_grads, axis=0), cosine, sine, True)
    grad_value_all = jnp.concatenate(value_grads, axis=0)
    grad_projected = (
        jnp.stack([grad_query_all, grad_key_all, grad_value_all], axis=1)
        .astype(jnp.bfloat16)
        .reshape(row_count, -1)
    )
    grad_qkv_part = jnp.dot(
        normed_low.T, grad_projected, preferred_element_type=jnp.float32
    ).reshape(D, 3, head_width)
    grad_one = lax.psum(
        jnp.dot(grad_projected, flat_qkv.T, preferred_element_type=jnp.float32).astype(
            jnp.bfloat16
        ),
        "heads",
    ).astype(jnp.float32)
    logits = jnp.dot(pooled, w_router, precision=highest, preferred_element_type=jnp.float32)
    logit_grads = []
    for group in range(2):
        group_logits = logits[:, LEVELS * group : LEVELS * (group + 1)]
        raised = jnp.exp(group_logits - jnp.max(group_logits, axis=1, keepdims=True))
        chosen = (jnp.arange(LEVELS)[None, :] == router_targets[:, group][:, None]).astype(
            jnp.float32
        )
        logit_grads.append(raised / jnp.sum(raised, axis=1, keepdims=True) - chosen)
    grad_logits = jnp.concatenate(logit_grads, axis=1)
    grad_router = jnp.dot(
        pooled.T, grad_logits, precision=highest, preferred_element_type=jnp.float32
    )
    grad_pooled = (
        jnp.dot(grad_logits, w_router.T, precision=highest, preferred_element_type=jnp.float32)
        * lax.rsqrt(seq_length)[:, None]
    )
    grad_one = grad_one + jnp.dot(
        member, grad_pooled, precision=highest, preferred_element_type=jnp.float32
    )
    back_one, grad_gain_one = normalize_back(grad_one, hat_one, inverse_one, gain_attn)
    grad_tokens = grad_hidden + back_one
    grad_qkv, grad_out, grad_gain_attn, grad_gain_ffn = (
        lax.psum(grad_qkv_part.astype(jnp.bfloat16), "seq").astype(jnp.float32),
        lax.psum(grad_out_part.astype(jnp.bfloat16), "seq").astype(jnp.float32),
        lax.psum(grad_gain_one.astype(jnp.bfloat16), "seq").astype(jnp.float32),
        lax.psum(grad_gain_two.astype(jnp.bfloat16), "seq").astype(jnp.float32),
    )
    return (
        output,
        grad_tokens,
        grad_qkv,
        grad_out,
        grad_up,
        grad_down,
        grad_gain_attn,
        grad_gain_ffn,
        grad_router,
    )


def solution(mesh):
    return jax.shard_map(
        local,
        mesh=mesh,
        in_specs=(
            P("seq", None),
            P(None, None, "heads"),
            P("heads", None),
            P("seq", "heads"),
            P("heads", "seq"),
            P(),
            P(),
            P(),
            P(),
            P(),
            P(),
            P("seq", None),
        ),
        out_specs=(
            P("seq", None),
            P("seq", None),
            P(None, None, "heads"),
            P("heads", None),
            P("seq", "heads"),
            P("heads", "seq"),
            P(),
            P(),
            P(),
        ),
        check_vma=False,
    )
```

profile of v0, /device:TPU:0, one launch (start us, length us, event | category | flops | bytes accessed | tf_op | source)
XLA Modules:
  0.0 1484.3 jit_solution(1231842556310068782)
XLA Ops:
  81.1 34.7 %all-gather.13.cloned.1.call-done = bf16[3,1024,512]{2,1,0:T(8,128)(2,1)} async-done(((bf16[3,128,512]{2,1,0:T(8,128)(2,1)}), bf16[3,1024,512]{2,1,0:T(8,128)(2,1)}) %all-gather.13.cloned.1.call-update) | async-done | bytes 3145744 | tf_op jit(solution)/shard_map/all_gather | solution.py:50
  134.2 29.5 %all-gather.17.cloned.1.call-done = bf16[2,2048,512]{2,1,0:T(8,128)(2,1)} async-done(((bf16[2,256,512]{2,1,0:T(8,128)(2,1)}), bf16[2,2048,512]{2,1,0:T(8,128)(2,1)}) %all-gather.17.cloned.1.call-update) | async-done | bytes 4194320 | tf_op jit(solution)/shard_map/all_gather | solution.py:50
  185.6 25.3 %all-gather.15.cloned.1.call-done = bf16[2,2048,512]{2,1,0:T(8,128)(2,1)} async-done(((bf16[2,256,512]{2,1,0:T(8,128)(2,1)}), bf16[2,2048,512]{2,1,0:T(8,128)(2,1)}) %all-gather.15.cloned.1.call-update) | async-done | bytes 4194320 | tf_op jit(solution)/shard_map/all_gather | solution.py:51
  240.7 153.0 %all-reduce.8.cloned.1.call-done = f32[896,2048]{1,0:T(8,128)} async-done(((f32[896,2048]{1,0:T(8,128)}), f32[896,2048]{1,0:T(8,128)}) %all-reduce.8.cloned.1.call-update) | async-done | bytes 7340048 | tf_op jit(solution)/shard_map/psum | solution.py:210
  402.5 74.7 %all-gather.19.cloned.1.call-done = bf16[2048,2048]{1,0:T(8,128)(2,1)} async-done(((bf16[256,2048]{1,0:T(8,128)(2,1)}), bf16[2048,2048]{1,0:T(8,128)(2,1)}) %all-gather.19.cloned.1.call-update) | async-done | bytes 8388624 | tf_op jit(solution)/shard_map/all_gather | solution.py:214
  477.2 14.6 fusion.154
  491.8 67.9 %all-gather.21.cloned.1.call-done = bf16[2048,2048]{1,0:T(8,128)(2,1)} async-done(((bf16[2048,256]{1,0:T(8,128)(2,1)}), bf16[2048,2048]{1,0:T(8,128)(2,1)}) %all-gather.21.cloned.1.call-update) | async-done | bytes 8388624 | tf_op jit(solution)/shard_map/all_gather | solution.py:215
  559.8 15.0 %fusion.29 = bf16[896,2048]{1,0:T(8,128)(2,1)} fusion(f32[896,2048]{1,0:T(8,128)} %fusion.154, s32[2048]{0:T(1024)S(1)} %iota_add_fusion, s32[896]{0:T(1024)S(1)} %broadcast_multiply_fusion, bf16[896,2048]{1,0:T(8,128)(2,1)} %param.23, bf16[2048,2048]{1,0:T(8,128)(2,1)} %all-gather.21.cloned.1.call-done), kind=kOutput, calls=%fused_computation.42 | convolution fusion | flops 7530872832 | bytes 23080448 | tf_op jit(solution)/shard_map/dot_general | solution.py:229
  593.4 146.5 %all-reduce.10.cloned.1.call-done = f32[896,2048]{1,0:T(8,128)} async-done(((f32[896,2048]{1,0:T(8,128)}), f32[896,2048]{1,0:T(8,128)}) %all-reduce.10.cloned.1.call-update) | async-done | bytes 7340048 | tf_op jit(solution)/shard_map/psum | solution.py:237
  760.6 15.4 %convolution_convert_fusion = bf16[2048,2048]{1,0:T(8,128)(2,1)} fusion(bf16[896,2048]{1,0:T(8,128)(2,1)} %param.23, f32[896,2048]{1,0:T(8,128)} %fusion.154, s32[2048]{0:T(1024)S(1)} %copy-done.58, s32[896]{0:T(1024)S(1)} %copy-done.63), kind=kOutput, calls=%fused_computation.31 | convolution fusion | flops 7529562112 | bytes 19410432 | tf_op jit(solution)/shard_map/dot_general | solution.py:235
  776.1 15.1 %convolution_convert_fusion.1 = bf16[2048,2048]{1,0:T(8,128)(2,1)} fusion(bf16[896,2048]{1,0:T(8,128)(2,1)} %fusion.29, f32[896,2048]{1,0:T(8,128)} %copy-done.3, f32[2048]{0:T(1024)S(1)} %copy-done.45, f32[896]{0:T(1024)S(1)} %add_rsqrt_fusion, f32[896]{0:T(1024)S(1)} %broadcast_multiply_fusion.6), kind=kOutput, calls=%fused_computation.32 | convolution fusion | flops 7527727104 | bytes 19414016 | tf_op jit(solution)/shard_map/dot_general | solution.py:236
  799.9 14.7 all_gather.51
  833.7 15.8 %all_gather.55 = f32[2,4,2048]{2,1,0:T(4,128)} all-gather(f32[2,4,256]{2,1,0:T(4,128)S(1)} %bitcast.162), channel_id=1, replica_groups=mesh['heads'=4,'seq'=8] {'seq'}, dimensions={2}, use_global_device_ids=true | all-gather | bytes 73728 | tf_op jit(solution)/shard_map/all_gather | solution.py:273
  872.7 13.8 multiply_reduce_fusion
  886.5 14.8 fusion.74
  901.6 15.1 %all_gather.53 = f32[3,4,1024]{2,1,0:T(4,128)S(1)} all-gather(f32[3,4,128]{2,1,0:T(4,128)S(1)} %get-tuple-element.61), channel_id=1, replica_groups=mesh['heads'=4,'seq'=8] {'seq'}, dimensions={2}, use_global_device_ids=true | all-gather | bytes 55296 | tf_op jit(solution)/shard_map/all_gather | solution.py:274
  916.7 15.4 %all_gather.57 = f32[2,4,2048]{2,1,0:T(4,128)} all-gather(f32[2,4,256]{2,1,0:T(4,128)S(1)} %get-tuple-element.59), channel_id=1, replica_groups=mesh['heads'=4,'seq'=8] {'seq'}, dimensions={2}, use_global_device_ids=true | all-gather | bytes 73728 | tf_op jit(solution)/shard_map/all_gather | solution.py:274
  966.0 13.0 fusion.72
  1010.4 15.1 %convolution_convert_fusion.3 = bf16[896,2048]{1,0:T(8,128)(2,1)} fusion(bf16[2048,2048]{1,0:T(8,128)(2,1)} %all-gather.21.cloned.1.call-done, f32[896,2048]{1,0:T(8,128)} %fusion.154, s32[2048]{0:T(1024)S(1)} %copy-done.59, s32[896]{0:T(1024)S(1)} %copy-done.64), kind=kOutput, calls=%fused_computation.73 | convolution fusion | flops 7527202816 | bytes 19410432 | tf_op jit(solution)/shard_map/dot_general | solution.py:219
  1041.9 28.2 %psum.67 = bf16[5,2048]{1,0:T(8,128)(2,1)S(1)} all-reduce(bf16[5,2048]{1,0:T(8,128)(2,1)S(1)} %fusion.55), channel_id=1, replica_groups=mesh['heads'=4,'seq'=8] {'seq'}, use_global_device_ids=true, to_apply=%region_18.19 | all-reduce | flops 10240 | bytes 40960 | tf_op jit(solution)/shard_map/psum | solution.py:189
  1074.9 22.1 %reduce-scatter.3.cloned.1.call-done = bf16[256,2048]{1,0:T(8,128)(2,1)} async-done(((bf16[2048,2048]{1,0:T(8,128)(2,1)}), bf16[256,2048]{1,0:T(8,128)(2,1)}) %reduce-scatter.3.cloned.1.call-update) | async-done | bytes 1048592 | tf_op jit(solution)/shard_map/reduce_scatter | solution.py:241
  1099.8 173.5 %all-reduce.12.cloned.1.call-done = (bf16[2048,3,512]{2,0,1:T(8,128)(2,1)}, bf16[512,2048]{1,0:T(8,128)(2,1)}) async-done(((bf16[2048,3,512]{2,0,1:T(8,128)(2,1)}, bf16[512,2048]{1,0:T(8,128)(2,1)}), (bf16[2048,3,512]{2,0,1:T(8,128)(2,1)}, bf16[512,2048]{1,0:T(8,128)(2,1)})) %all-reduce.12.cloned.1.call-update) | async-done | bytes 8388624 | tf_op jit(solution)/shard_map/psum | solution.py:322
  1284.8 148.0 %all-reduce.14.cloned.1.call-done = (bf16[896,2048]{1,0:T(8,128)(2,1)}, bf16[896,2048]{1,0:T(8,128)(2,1)}) async-done(((bf16[896,2048]{1,0:T(8,128)(2,1)}, bf16[896,2048]{1,0:T(8,128)(2,1)}), (bf16[896,2048]{1,0:T(8,128)(2,1)}, bf16[896,2048]{1,0:T(8,128)(2,1)})) %all-reduce.14.cloned.1.call-update) | async-done | bytes 7340048 | tf_op jit(solution)/shard_map/psum | solution.py:220
  1449.5 16.5 %all-reduce = (bf16[2048]{0:T(1024)(128)(2,1)S(1)}, bf16[2048]{0:T(1024)(128)(2,1)S(1)}) all-reduce(bf16[2048]{0:T(1024)(128)(2,1)S(1)} %get-tuple-element.11, bf16[2048]{0:T(1024)(128)(2,1)S(1)} %copy-done.52), channel_id=1, replica_groups=mesh['heads'=4,'seq'=8] {'seq'}, use_global_device_ids=true, to_apply=%region_30.31 | all-reduce | flops 4096 | bytes 16384 | tf_op jit(solution)/shard_map/psum | solution.py:324
  (311 shorter events, 371.6 us)
Async XLA Ops:
  7.2 225.8 %copy-start = (bf16[512,2048]{1,0:T(8,128)(2,1)S(1)}, bf16[512,2048]{1,0:T(8,128)(2,1)}, u32[]{:S(2)}) copy-start(bf16[512,2048]{1,0:T(8,128)(2,1)} %param.14) | copy-start | bytes 6291460
  7.2 69.3 %all-gather.11.cloned.1.call-start = ((), (), s32[]{:S(2)}) async-start(), calls=%async_computation.2 | async-start | bytes 3538944 | tf_op jit(solution)/shard_map/all_gather | solution.py:51
  35.4 80.4 %all-gather.13.cloned.1.call-start = ((), (), s32[]{:S(2)}) async-start(), calls=%async_computation.3 | async-start | bytes 3538944 | tf_op jit(solution)/shard_map/all_gather | solution.py:50
  57.9 105.9 %all-gather.17.cloned.1.call-start = ((), (), s32[]{:S(2)}) async-start(), calls=%async_computation.5 | async-start | bytes 4718592 | tf_op jit(solution)/shard_map/all_gather | solution.py:50
  61.7 149.3 %all-gather.15.cloned.1.call-start = ((), (), s32[]{:S(2)}) async-start(), calls=%async_computation.4 | async-start | bytes 4718592 | tf_op jit(solution)/shard_map/all_gather | solution.py:51
  63.6 330.0 %all-reduce.8.cloned.1.call-start = ((), (), s32[]{:S(2)}) async-start(), calls=%async_computation.6 | async-start | bytes 14680064 | tf_op jit(solution)/shard_map/psum | solution.py:210
  63.9 168.0 %copy-start.69 = (s32[512]{0:T(512)}, s32[512]{0:T(512)S(1)}, u32[]{:S(2)}) copy-start(s32[512]{0:T(512)S(1)} %fusion.125) | copy-start | bytes 6148
  68.7 163.3 %copy-start.65 = (s32[896]{0:T(1024)}, s32[896]{0:T(1024)S(1)}, u32[]{:S(2)}) copy-start(s32[896]{0:T(1024)S(1)} %broadcast_multiply_fusion.1) | copy-start | bytes 10756
  68.8 57.0 %copy-start.11 = (pred[128,1024]{1,0:T(8,128)(4,1)}, pred[128,1024]{1,0:T(8,128)(4,1)S(1)}, u32[]{:S(2)}) copy-start(pred[128,1024]{1,0:T(8,128)(4,1)S(1)} %iota_compare_fusion.3) | copy-start | bytes 393220
  239.3 237.9 %all-gather.19.cloned.1.call-start = ((), (), s32[]{:S(2)}) async-start(), calls=%async_computation.7 | async-start | bytes 9437184 | tf_op jit(solution)/shard_map/all_gather | solution.py:214
  239.8 319.9 %all-gather.21.cloned.1.call-start = ((), (), s32[]{:S(2)}) async-start(), calls=%async_computation.8 | async-start | bytes 9437184 | tf_op jit(solution)/shard_map/all_gather | solution.py:215
  240.6 499.3 %all-reduce.10.cloned.1.call-start = ((), (), s32[]{:S(2)}) async-start(), calls=%async_computation.9 | async-start | bytes 14680064 | tf_op jit(solution)/shard_map/psum | solution.py:237
  240.7 319.1 %copy-start.57 = (s32[2048]{0:T(1024)}, s32[2048]{0:T(1024)S(1)}, u32[]{:S(2)}) copy-start(s32[2048]{0:T(1024)S(1)} %iota_add_fusion) | copy-start | bytes 24580
  240.7 319.1 %copy-start.62 = (s32[896]{0:T(1024)}, s32[896]{0:T(1024)S(1)}, u32[]{:S(2)}) copy-start(s32[896]{0:T(1024)S(1)} %broadcast_multiply_fusion) | copy-start | bytes 10756
  398.6 78.6 %copy-start.44 = (f32[2048]{0:T(1024)S(1)}, f32[2048]{0:T(1024)}, u32[]{:S(2)}) copy-start(f32[2048]{0:T(1024)} %param.18) | copy-start | bytes 24580
  586.1 209.2 %all-gather.23.cloned.1.call-start = ((), (), s32[]{:S(2)}) async-start(), calls=%async_computation.10 | async-start | bytes 3538944 | tf_op jit(solution)/shard_map/all_gather | solution.py:269
  590.0 237.3 %all-gather.27.cloned.1.call-start = ((), (), s32[]{:S(2)}) async-start(), calls=%async_computation.12 | async-start | bytes 4718592 | tf_op jit(solution)/shard_map/all_gather | solution.py:269
  593.3 154.0 %copy-start.45 = (f32[2048]{0:T(1024)S(1)}, f32[2048]{0:T(1024)}, u32[]{:S(2)}) copy-start(f32[2048]{0:T(1024)} %param.18) | copy-start | bytes 24580
  593.3 346.1 %all-gather.25.cloned.1.call-start = ((), (), s32[]{:S(2)}) async-start(), calls=%async_computation.11 | async-start | bytes 3538944 | tf_op jit(solution)/shard_map/all_gather | solution.py:270
  758.4 197.6 %all-gather.29.cloned.1.call-start = ((), (), s32[]{:S(2)}) async-start(), calls=%async_computation.13 | async-start | bytes 4718592 | tf_op jit(solution)/shard_map/all_gather | solution.py:270
  760.6 311.6 %reduce-scatter.5.cloned.1.call-start = ((), (), s32[]{:S(2)}) async-start(), calls=%async_computation.15 | async-start | bytes 9437184 | tf_op jit(solution)/shard_map/reduce_scatter | solution.py:244
  776.1 320.9 %reduce-scatter.3.cloned.1.call-start = ((), (), s32[]{:S(2)}) async-start(), calls=%async_computation.14 | async-start | bytes 9437184 | tf_op jit(solution)/shard_map/reduce_scatter | solution.py:241
  791.3 482.0 %all-reduce.12.cloned.1.call-start = ((), (), s32[]{:S(2)}) async-start(), calls=%async_computation.16 | async-start | bytes 16777216 | tf_op jit(solution)/shard_map/psum | solution.py:322
  1009.7 423.1 %all-reduce.14.cloned.1.call-start = ((), (), s32[]{:S(2)}) async-start(), calls=%async_computation.17 | async-start | bytes 14680064 | tf_op jit(solution)/shard_map/psum | solution.py:220
  (66 other events, 647.8 us)
Sparse Core Ops, SparseCore 0:
  35.5 40.9 all-gather.10
  78.6 37.1 all-gather.12
  118.0 45.7 all-gather.16
  165.2 45.6 all-gather.14
  239.4 154.2 all-reduce.7
  395.1 82.0 all-gather.18
  478.7 80.9 all-gather.20
  586.2 153.6 all-reduce.9
  741.5 38.1 all-gather.22
  781.2 46.1 all-gather.26
  829.0 40.0 all-gather.24
  871.1 44.4 all-gather.28
  917.9 87.9 reduce-scatter.4
  1008.6 88.2 reduce-scatter.2
  1099.2 174.0 all-reduce.11
  1277.2 155.5 all-reduce.13
where the time goes:
time: 1490 us; the launch traced here: 1480 us
  waiting for transfers between devices  891 us (60%)
  matrix products  268 us (18%)
  local copies, waits for them, and re-layouts  115 us (8%)
  blocking collectives  106 us (7%)
  other arithmetic  88.5 us (6%)
  between operations  15.1 us (1%)
    psum x1, waiting for transfers between devices, local(): lax.psum(grad_qkv_part.astype(jnp.bfloat16), 'seq').astype(jnp.float32)  174 us
    psum x1, waiting for transfers between devices, local(): hidden = tokens_wide + lax.psum(attn_part, 'heads')  153 us
    psum x1, waiting for transfers between devices, local(): lax.psum(ffn_part.astype(jnp.bfloat16), 'heads').astype(jnp.float32)  148 us
    psum x1, waiting for transfers between devices, local(): lax.psum(jnp.dot(grad_upward, back_up.T, preferred_element_type=jnp.float...  146 us
    all_gather x1, waiting for transfers between devices, local(): lax.all_gather(w_up, 'seq', axis=0, tiled=True)  74.7 us
    all_gather x1, waiting for transfers between devices, local(): lax.all_gather(w_down, 'seq', axis=1, tiled=True)  67.9 us
    all_gather x2, waiting for transfers between devices, gather_rows(): lax.all_gather(keys, 'seq', axis=1, tiled=True)  64.2 us
    unnamed x153, local copies, waits for them, and re-layouts  34.3 us
  transfers between devices with their start and end apart: 16, of which 12 were waited for; matrix products, arithmetic and copies ran while one was open for 23% of the time, Pallas kernels for 0%

commit v1 on v0

--- a/solution.py
+++ b/solution.py
@@ -2,6 +2,7 @@
 import jax.numpy as jnp
 from jax import lax
 from jax.sharding import PartitionSpec as P
+from jax.lax import axis_index, axis_size, ppermute
 
 D = 2048
 H = 16
@@ -14,6 +15,21 @@
 SEQS = 5
 epsilon = 1e-05
 highest = lax.Precision.HIGHEST
+
+
+def enter_samples(chunk):
+    axis_total = axis_size("seq")
+    in_order = list(map(lambda hop_no: (hop_no, (hop_no + 1) % axis_total), range(axis_total)))
+    sides = list(map(lambda hop_no: (hop_no, (hop_no - 1) % axis_total), range(axis_total)))
+    s_next, next_value = ([chunk], [chunk])
+    for _ in range(axis_total // 2):
+        s_next.append(ppermute(s_next[-1], axis_name="seq", perm=in_order))
+    k0 = 0
+    while k0 < (axis_total - 1) // 2:
+        next_value.append(ppermute(next_value[-1], axis_name="seq", perm=sides))
+        k0 = k0 + 1
+    y = jnp.concatenate([*s_next[::-1], *next_value[1:]], 0)
+    return jnp.roll(y, (axis_index("seq") - axis_total // 2) * chunk.shape[0], 0)
 
 
 def normalize_parts(values):
@@ -210,10 +226,7 @@
     hidden = tokens_wide + lax.psum(attn_part, "heads")
     hat_two, inverse_two = normalize_parts(hidden)
     normed_two = (hat_two * gain_ffn).astype(jnp.bfloat16)
-    full_up, full_down = (
-        lax.all_gather(w_up, "seq", axis=0, tiled=True),
-        lax.all_gather(w_down, "seq", axis=1, tiled=True),
-    )
+    full_up, full_down = (enter_samples(w_up), lax.all_gather(w_down, "seq", axis=1, tiled=True))
     upward = jnp.dot(normed_two, full_up, preferred_element_type=jnp.float32)
     active = (jnp.square(jnp.maximum(upward, 0.0)) * ffn_live).astype(jnp.bfloat16)
     ffn_part = jnp.dot(active, full_down, preferred_element_type=jnp.float32)

time: 1490 us -> 1560 us (1.047)
  local copies, waits for them, and re-layouts: 115 us -> 142 us
  waiting for transfers between devices: 891 us -> 910 us
    ppermute x0 -> x7, waiting for transfers between devices: none -> 122 us  [the longest x4 118 us: enter_samples(): s_next.append(ppermute(s_next[-1], axis_name='seq', perm=in_order))]
    psum x1, waiting for transfers between devices: 174 us -> 97.7 us  [local(): lax.psum(grad_qkv_part.astype(jnp.bfloat16), 'seq').astype(jnp.float32)]
    unnamed x153 -> x178, local copies, waits for them, and re-layouts: 34.3 us -> 63.8 us
    reduce_scatter x1, waiting for transfers between devices: 22.1 us -> 0.01 us  [local(): lax.psum_scatter(grad_up_part.astype(jnp.bfloat16), 'seq', scatter_dimens...]
  transfers between devices with their start and end apart: 16 -> 23, of which waited for: 12 -> 15; matrix products, arithmetic and copies ran while one was open for 23% -> 24% of each run, Pallas kernels for 0% -> 0%
where the time goes in v1:
time: 1560 us; the launch traced here: 1550 us
  waiting for transfers between devices  910 us (58%)
  matrix products  273 us (18%)
  local copies, waits for them, and re-layouts  142 us (9%)
  blocking collectives  107 us (7%)
  other arithmetic  93 us (6%)
    psum x1, waiting for transfers between devices, local(): hidden = tokens_wide + lax.psum(attn_part, 'heads')  153 us
    psum x1, waiting for transfers between devices, local(): lax.psum(jnp.dot(grad_upward, back_up.T, preferred_element_type=jnp.float...  150 us
    psum x1, waiting for transfers between devices, local(): lax.psum(ffn_part.astype(jnp.bfloat16), 'heads').astype(jnp.float32)  148 us
    ppermute x4, waiting for transfers between devices, enter_samples(): s_next.append(ppermute(s_next[-1], axis_name='seq', perm=in_order))  118 us
    psum x1, waiting for transfers between devices, local(): lax.psum(grad_qkv_part.astype(jnp.bfloat16), 'seq').astype(jnp.float32)  97.7 us
    all_gather x1, waiting for transfers between devices, local(): lax.all_gather(w_up, 'seq', axis=0, tiled=True)  72.7 us
    all_gather x1, waiting for transfers between devices, local(): lax.all_gather(w_down, 'seq', axis=1, tiled=True)  69.5 us
    all_gather x2, waiting for transfers between devices, gather_rows(): lax.all_gather(keys, 'seq', axis=1, tiled=True)  64.2 us
  transfers between devices with their start and end apart: 23, of which 15 were waited for; matrix products, arithmetic and copies ran while one was open for 24% of the time, Pallas kernels for 0%

profile of v1, /device:TPU:0, one launch (start us, length us, event | category | flops | bytes accessed | tf_op | source)
XLA Modules:
  0.0 1551.7 jit_solution(1811007774868459381)
XLA Ops:
  81.2 34.6 %all-gather.13.cloned.1.call-done = bf16[3,1024,512]{2,1,0:T(8,128)(2,1)} async-done(((bf16[3,128,512]{2,1,0:T(8,128)(2,1)}), bf16[3,1024,512]{2,1,0:T(8,128)(2,1)}) %all-gather.13.cloned.1.call-update) | async-done | bytes 3145744 | tf_op jit(solution)/shard_map/all_gather | solution.py:66
  134.2 29.5 %all-gather.17.cloned.1.call-done = bf16[2,2048,512]{2,1,0:T(8,128)(2,1)} async-done(((bf16[2,256,512]{2,1,0:T(8,128)(2,1)}), bf16[2,2048,512]{2,1,0:T(8,128)(2,1)}) %all-gather.17.cloned.1.call-update) | async-done | bytes 4194320 | tf_op jit(solution)/shard_map/all_gather | solution.py:66
  185.7 25.3 %all-gather.15.cloned.1.call-done = bf16[2,2048,512]{2,1,0:T(8,128)(2,1)} async-done(((bf16[2,256,512]{2,1,0:T(8,128)(2,1)}), bf16[2,2048,512]{2,1,0:T(8,128)(2,1)}) %all-gather.15.cloned.1.call-update) | async-done | bytes 4194320 | tf_op jit(solution)/shard_map/all_gather | solution.py:67
  240.8 152.9 %all-reduce.8.cloned.1.call-done = f32[896,2048]{1,0:T(8,128)} async-done(((f32[896,2048]{1,0:T(8,128)}), f32[896,2048]{1,0:T(8,128)}) %all-reduce.8.cloned.1.call-update) | async-done | bytes 7340048 | tf_op jit(solution)/shard_map/psum | solution.py:226
  404.6 72.7 %all-gather.21.cloned.1.call-done = bf16[2048,2048]{1,0:T(8,128)(2,1)} async-done(((bf16[256,2048]{1,0:T(8,128)(2,1)}), bf16[2048,2048]{1,0:T(8,128)(2,1)}) %all-gather.21.cloned.1.call-update) | async-done | bytes 8388624 | tf_op jit(solution)/shard_map/all_gather | solution.py:237
  490.3 69.5 %all-gather.19.cloned.1.call-done = bf16[2048,2048]{1,0:T(8,128)(2,1)} async-done(((bf16[2048,256]{1,0:T(8,128)(2,1)}), bf16[2048,2048]{1,0:T(8,128)(2,1)}) %all-gather.19.cloned.1.call-update) | async-done | bytes 8388624 | tf_op jit(solution)/shard_map/all_gather | solution.py:229
  559.8 15.0 fusion.31
  590.0 150.0 %all-reduce.10.cloned.1.call-done = f32[896,2048]{1,0:T(8,128)} async-done(((f32[896,2048]{1,0:T(8,128)}), f32[896,2048]{1,0:T(8,128)}) %all-reduce.10.cloned.1.call-update) | async-done | bytes 7340048 | tf_op jit(solution)/shard_map/psum | solution.py:250
  758.7 15.3 convolution_convert_fusion
  775.3 16.1 %collective-permute-done = bf16[256,2048]{1,0:T(8,128)(2,1)S(1)} collective-permute-done((bf16[256,2048]{1,0:T(8,128)(2,1)S(1)}, bf16[256,2048]{1,0:T(8,128)(2,1)S(1)}, u32[]{:S(2)}, u32[]{:S(2)}) %collective-permute-start) | collective-permute-done | bytes 1048608 | tf_op jit(solution)/shard_map/ppermute | solution.py:26
  794.9 46.1 %collective-permute-done.1 = bf16[256,2048]{1,0:T(8,128)(2,1)S(1)} collective-permute-done((bf16[256,2048]{1,0:T(8,128)(2,1)S(1)}, bf16[256,2048]{1,0:T(8,128)(2,1)S(1)}, u32[]{:S(2)}, u32[]{:S(2)}) %collective-permute-start.1) | collective-permute-done | bytes 1048608 | tf_op jit(solution)/shard_map/ppermute | solution.py:26
  844.6 24.3 %collective-permute-done.2 = bf16[256,2048]{1,0:T(8,128)(2,1)} collective-permute-done((bf16[256,2048]{1,0:T(8,128)(2,1)S(1)}, bf16[256,2048]{1,0:T(8,128)(2,1)}, u32[]{:S(2)}, u32[]{:S(2)}) %collective-permute-start.2) | collective-permute-done | bytes 1048608 | tf_op jit(solution)/shard_map/ppermute | solution.py:26
  880.4 31.5 %collective-permute-done.3 = bf16[256,2048]{1,0:T(8,128)(2,1)} collective-permute-done((bf16[256,2048]{1,0:T(8,128)(2,1)}, bf16[256,2048]{1,0:T(8,128)(2,1)}, u32[]{:S(2)}, u32[]{:S(2)}) %collective-permute-start.3) | collective-permute-done | bytes 1048608 | tf_op jit(solution)/shard_map/ppermute | solution.py:26
  960.0 19.8 %all_gather.50 = f32[3,4,1024]{2,1,0:T(4,128)S(1)} all-gather(f32[3,4,128]{2,1,0:T(4,128)S(1)} %log_add_fusion.1), channel_id=1, replica_groups=mesh['heads'=4,'seq'=8] {'seq'}, dimensions={2}, use_global_device_ids=true | all-gather | bytes 55296 | tf_op jit(solution)/shard_map/all_gather | solution.py:286
  992.0 14.4 all_gather.54
  1029.6 13.4 multiply_reduce_fusion
  1043.0 14.8 fusion.91
  1071.3 14.4 all_gather.56
  1120.6 13.6 fusion.89
  1165.6 24.3 %fusion.54 = bf16[896,2048]{1,0:T(8,128)(2,1)} fusion(bf16[2048,2048]{1,0:T(8,128)(2,1)} %all-gather.19.cloned.1.call-done, bf16[896,2048]{1,0:T(8,128)(2,1)} %multiply_convert_fusion.4, bf16[4096,2048]{1,0:T(8,128)(2,1)} %constant_dynamic-update-slice_fusion, s32[]{:T(128)S(6)} %select_n.135, s32[2048]{0:T(1024)S(1)} %copy-done.61, s32[896]{0:T(1024)S(1)} %copy-done.65), kind=kOutput, calls=%fused_computation.83 | convolution fusion | flops 15043395584 | bytes 24129028 | tf_op jit(solution)/shard_map/dot_general | solution.py:232
  1206.3 29.1 %psum.67 = bf16[5,2048]{1,0:T(8,128)(2,1)S(1)} all-reduce(bf16[5,2048]{1,0:T(8,128)(2,1)S(1)} %fusion.72), channel_id=1, replica_groups=mesh['heads'=4,'seq'=8] {'seq'}, use_global_device_ids=true, to_apply=%region_18.19 | all-reduce | flops 10240 | bytes 40960 | tf_op jit(solution)/shard_map/psum | solution.py:205
  1242.9 97.7 %all-reduce.12.cloned.1.call-done = (bf16[2048,3,512]{2,0,1:T(8,128)(2,1)}, bf16[512,2048]{1,0:T(8,128)(2,1)}) async-done(((bf16[2048,3,512]{2,0,1:T(8,128)(2,1)}, bf16[512,2048]{1,0:T(8,128)(2,1)}), (bf16[2048,3,512]{2,0,1:T(8,128)(2,1)}, bf16[512,2048]{1,0:T(8,128)(2,1)})) %all-reduce.12.cloned.1.call-update) | async-done | bytes 8388624 | tf_op jit(solution)/shard_map/psum | solution.py:335
  1352.1 148.0 %all-reduce.14.cloned.1.call-done = (bf16[896,2048]{1,0:T(8,128)(2,1)}, bf16[896,2048]{1,0:T(8,128)(2,1)}) async-done(((bf16[896,2048]{1,0:T(8,128)(2,1)}, bf16[896,2048]{1,0:T(8,128)(2,1)}), (bf16[896,2048]{1,0:T(8,128)(2,1)}, bf16[896,2048]{1,0:T(8,128)(2,1)})) %all-reduce.14.cloned.1.call-update) | async-done | bytes 7340048 | tf_op jit(solution)/shard_map/psum | solution.py:233
  1516.9 16.5 %all-reduce = (bf16[2048]{0:T(1024)(128)(2,1)S(1)}, bf16[2048]{0:T(1024)(128)(2,1)S(1)}) all-reduce(bf16[2048]{0:T(1024)(128)(2,1)S(1)} %get-tuple-element.11, bf16[2048]{0:T(1024)(128)(2,1)S(1)} %copy-done.53), channel_id=1, replica_groups=mesh['heads'=4,'seq'=8] {'seq'}, use_global_device_ids=true, to_apply=%region_30.31 | all-reduce | flops 4096 | bytes 16384 | tf_op jit(solution)/shard_map/psum | solution.py:337
  (352 shorter events, 447.5 us)
Async XLA Ops:
  7.2 69.3 %all-gather.11.cloned.1.call-start = ((), (), s32[]{:S(2)}) async-start(), calls=%async_computation.2 | async-start | bytes 3538944 | tf_op jit(solution)/shard_map/all_gather | solution.py:67
  35.4 80.4 %all-gather.13.cloned.1.call-start = ((), (), s32[]{:S(2)}) async-start(), calls=%async_computation.3 | async-start | bytes 3538944 | tf_op jit(solution)/shard_map/all_gather | solution.py:66
  57.9 105.9 %all-gather.17.cloned.1.call-start = ((), (), s32[]{:S(2)}) async-start(), calls=%async_computation.5 | async-start | bytes 4718592 | tf_op jit(solution)/shard_map/all_gather | solution.py:66
  61.6 149.3 %all-gather.15.cloned.1.call-start = ((), (), s32[]{:S(2)}) async-start(), calls=%async_computation.4 | async-start | bytes 4718592 | tf_op jit(solution)/shard_map/all_gather | solution.py:67
  63.6 330.1 %all-reduce.8.cloned.1.call-start = ((), (), s32[]{:S(2)}) async-start(), calls=%async_computation.6 | async-start | bytes 14680064 | tf_op jit(solution)/shard_map/psum | solution.py:226
  239.4 237.9 %all-gather.21.cloned.1.call-start = ((), (), s32[]{:S(2)}) async-start(), calls=%async_computation.8 | async-start | bytes 9437184 | tf_op jit(solution)/shard_map/all_gather | solution.py:237
  239.9 319.9 %all-gather.19.cloned.1.call-start = ((), (), s32[]{:S(2)}) async-start(), calls=%async_computation.7 | async-start | bytes 9437184 | tf_op jit(solution)/shard_map/all_gather | solution.py:229
  240.7 499.3 %all-reduce.10.cloned.1.call-start = ((), (), s32[]{:S(2)}) async-start(), calls=%async_computation.9 | async-start | bytes 14680064 | tf_op jit(solution)/shard_map/psum | solution.py:250
  240.8 319.1 %copy-start.59 = (s32[2048]{0:T(1024)}, s32[2048]{0:T(1024)S(1)}, u32[]{:S(2)}) copy-start(s32[2048]{0:T(1024)S(1)} %iota_add_fusion) | copy-start | bytes 24580
  586.2 369.1 %all-gather.23.cloned.1.call-start = ((), (), s32[]{:S(2)}) async-start(), calls=%async_computation.10 | async-start | bytes 3538944 | tf_op jit(solution)/shard_map/all_gather | solution.py:282
  588.4 397.1 %all-gather.27.cloned.1.call-start = ((), (), s32[]{:S(2)}) async-start(), calls=%async_computation.12 | async-start | bytes 4718592 | tf_op jit(solution)/shard_map/all_gather | solution.py:282
  589.9 503.4 %all-gather.25.cloned.1.call-start = ((), (), s32[]{:S(2)}) async-start(), calls=%async_computation.11 | async-start | bytes 3538944 | tf_op jit(solution)/shard_map/all_gather | solution.py:283
  757.5 352.4 %all-gather.29.cloned.1.call-start = ((), (), s32[]{:S(2)}) async-start(), calls=%async_computation.13 | async-start | bytes 4718592 | tf_op jit(solution)/shard_map/all_gather | solution.py:283
  758.6 478.8 %reduce-scatter.5.cloned.1.call-start = ((), (), s32[]{:S(2)}) async-start(), calls=%async_computation.15 | async-start | bytes 9437184 | tf_op jit(solution)/shard_map/reduce_scatter | solution.py:257
  774.1 466.0 %reduce-scatter.3.cloned.1.call-start = ((), (), s32[]{:S(2)}) async-start(), calls=%async_computation.14 | async-start | bytes 9437184 | tf_op jit(solution)/shard_map/reduce_scatter | solution.py:254
  775.3 16.1 %collective-permute-start = (bf16[256,2048]{1,0:T(8,128)(2,1)S(1)}, bf16[256,2048]{1,0:T(8,128)(2,1)S(1)}, u32[]{:S(2)}, u32[]{:S(2)}) collective-permute-start(bf16[256,2048]{1,0:T(8,128)(2,1)S(1)} %copy-done.15), channel_id=1, source_target_pairs={{0,1},{1,2},{2,3},{3,4},{4,5},{5,6},{6,7},{7,0},{8,9},{9,10},{10,1... | collective-permute-start | bytes 3145736 | tf_op jit(solution)/shard_map/ppermute | solution.py:26
  791.4 49.7 %collective-permute-start.1 = (bf16[256,2048]{1,0:T(8,128)(2,1)S(1)}, bf16[256,2048]{1,0:T(8,128)(2,1)S(1)}, u32[]{:S(2)}, u32[]{:S(2)}) collective-permute-start(bf16[256,2048]{1,0:T(8,128)(2,1)S(1)} %collective-permute-done), channel_id=1, source_target_pairs={{0,1},{1,2},{2,3},{3,4},{4,5},{5,6},{6,7},{7,0},{8,9},{9,10},{10,1... | collective-permute-start | bytes 3145736 | tf_op jit(solution)/shard_map/ppermute | solution.py:26
  791.4 49.7 %collective-permute-start.4 = (bf16[256,2048]{1,0:T(8,128)(2,1)S(1)}, bf16[256,2048]{1,0:T(8,128)(2,1)}, u32[]{:S(2)}, u32[]{:S(2)}) collective-permute-start(bf16[256,2048]{1,0:T(8,128)(2,1)S(1)} %copy-done.15), channel_id=1, source_target_pairs={{0,7},{1,0},{2,1},{3,2},{4,3},{5,4},{6,5},{7,6},{8,15},{9,8},{10,9... | collective-permute-start | bytes 3145736 | tf_op jit(solution)/shard_map/ppermute | solution.py:29
  841.1 27.8 %collective-permute-start.2 = (bf16[256,2048]{1,0:T(8,128)(2,1)S(1)}, bf16[256,2048]{1,0:T(8,128)(2,1)}, u32[]{:S(2)}, u32[]{:S(2)}) collective-permute-start(bf16[256,2048]{1,0:T(8,128)(2,1)S(1)} %collective-permute-done.1), channel_id=1, source_target_pairs={{0,1},{1,2},{2,3},{3,4},{4,5},{5,6},{6,7},{7,0},{8,9},{9,10},{10,1... | collective-permute-start | bytes 3145736 | tf_op jit(solution)/shard_map/ppermute | solution.py:26
  842.0 34.7 %collective-permute-start.5 = (bf16[256,2048]{1,0:T(8,128)(2,1)}, bf16[256,2048]{1,0:T(8,128)(2,1)}, u32[]{:S(2)}, u32[]{:S(2)}) collective-permute-start(bf16[256,2048]{1,0:T(8,128)(2,1)} %collective-permute-done.4), channel_id=1, source_target_pairs={{0,7},{1,0},{2,1},{3,2},{4,3},{5,4},{6,5},{7,6},{8,15},{9,8},{10,9... | collective-permute-start | bytes 3145736 | tf_op jit(solution)/shard_map/ppermute | solution.py:29
  868.9 43.1 %collective-permute-start.3 = (bf16[256,2048]{1,0:T(8,128)(2,1)}, bf16[256,2048]{1,0:T(8,128)(2,1)}, u32[]{:S(2)}, u32[]{:S(2)}) collective-permute-start(bf16[256,2048]{1,0:T(8,128)(2,1)} %collective-permute-done.2), channel_id=1, source_target_pairs={{0,1},{1,2},{2,3},{3,4},{4,5},{5,6},{6,7},{7,0},{8,9},{9,10},{10,1... | collective-permute-start | bytes 3145736 | tf_op jit(solution)/shard_map/ppermute | solution.py:26
  876.7 61.2 %collective-permute-start.6 = (bf16[256,2048]{1,0:T(8,128)(2,1)}, bf16[256,2048]{1,0:T(8,128)(2,1)}, u32[]{:S(2)}, u32[]{:S(2)}) collective-permute-start(bf16[256,2048]{1,0:T(8,128)(2,1)} %collective-permute-done.5), channel_id=1, source_target_pairs={{0,7},{1,0},{2,1},{3,2},{4,3},{5,4},{6,5},{7,6},{8,15},{9,8},{10,9... | collective-permute-start | bytes 3145736 | tf_op jit(solution)/shard_map/ppermute | solution.py:29
  937.8 402.8 %all-reduce.12.cloned.1.call-start = ((), (), s32[]{:S(2)}) async-start(), calls=%async_computation.16 | async-start | bytes 16777216 | tf_op jit(solution)/shard_map/psum | solution.py:335
  1165.0 335.2 %all-reduce.14.cloned.1.call-start = ((), (), s32[]{:S(2)}) async-start(), calls=%async_computation.17 | async-start | bytes 14680064 | tf_op jit(solution)/shard_map/psum | solution.py:233
  (78 other events, 1719.5 us)
Sparse Core Ops, SparseCore 0:
  35.5 40.9 all-gather.10
  78.7 37.1 all-gather.12
  118.0 45.7 all-gather.16
  165.2 45.6 all-gather.14
  239.5 154.2 all-reduce.7
  395.2 82.0 all-gather.20
  478.8 80.9 all-gather.18
  586.3 153.6 all-reduce.9
  741.6 38.1 all-gather.22
  781.3 67.3 all-gather.26
  850.3 61.2 all-gather.24
  913.1 47.7 all-gather.28
  963.1 88.6 reduce-scatter.4
  1054.5 88.9 reduce-scatter.2
  1165.1 175.4 all-reduce.11
  1344.6 155.5 all-reduce.13
